TPU v7x, 256 devices: a whole 4x4x8 slice. The times are simulated.
256 devices in a mesh: seq: 32 (over z_hi, x, core), exp: 8 (over z_lo, y).
Axes of the slice: x: 4, y: 4, z: 8 (z_hi: 4, z_lo: 2; z = z_hi * 2 + z_lo), core: 2. Of those that a mesh axis runs over, the one named last changes fastest.
Arguments:
- tokens: bfloat16 [4096, 2304], P('seq'), may hold values from -6 to 6
- norm_gain: bfloat16 [2304], replicated, may hold values from 0.099609375 to 1.8984375
- w_qkv: bfloat16 [2304, 3, 2048], P(None, None, 'exp'), may hold values from -12 to 12
- w_out: bfloat16 [2048, 2304], P('exp'), may hold values from -0.125 to 0.125
- moe_gain: bfloat16 [2304], replicated, may hold values from 0.099609375 to 1.8984375
- w_router: bfloat16 [2304, 8], replicated, may hold values from -0.25 to 0.25
- gate_up: bfloat16 [8, 2, 2304, 5760], P('exp', None, None, 'seq'), may hold values from -0.125 to 0.125
- w_down: bfloat16 [8, 5760, 2304], P('exp', 'seq'), may hold values from -0.078125 to 0.078125
- lengths: int32 [4], replicated, may hold values from 1 to 3072, as said below
- blocks_seen: int32 [32, 32], P('seq'), may hold values from 0 to 1, as said below
- expert_ids: int32 [4096, 2], P(('seq', 'exp')), may hold values from 0 to 7, all different within a row; in each aligned block of 16 rows (0 to 15, 16 to 31, ...) at most 8 rows name the same one
- old_place: int32 [8], replicated, may hold values from 0 to 7, each once
- new_place: int32 [8], replicated, may hold values from 0 to 7, each once
Outputs:
- layer_out: bfloat16 [4096, 2304], P(('seq', 'exp'))
- new_gate_up: bfloat16 [8, 2, 2304, 5760], P('exp', None, None, 'seq')
- new_down: bfloat16 [8, 5760, 2304], P('exp', 'seq')
Inputs may be any that keep to these rules, and one draw needn't show every extreme that they name: `lengths`: positive, summing to 4096, the largest exactly 3072. `blocks_seen`: 1 on the diagonal; 0 above it and wherever no sequence has tokens in both blocks; elsewhere 0 or 1. `expert_ids`: the two experts of a token differ; among the 16 tokens of one device no expert is named more than 8 times, and in some devices one expert exactly 8 times. `old_place`: a permutation of the experts. `new_place`: a permutation of the experts.
All inputs are finite; a program needn't handle non-finite values.
Results may differ from a plain program's by a relative error of at most 0.023.
Values may be sent and summed in bfloat16 or wider, within the bound.
No kernel may reach another device: no remote copies, remote signals or barrier semaphores. Data moves between devices by JAX's collectives and lax.ppermute only.
A program may use at most 128 MiB of HBM per device.

v0:
```python
import jax
import jax.numpy as jnp
from jax import lax
from jax.sharding import PartitionSpec as P

HEAD_DIM = 64
epsilon = 1e-05
masked_score = -1e30


def rms_scale(values_in, gain):
    widened = values_in.astype(jnp.float32)
    inverse = lax.rsqrt(jnp.mean(widened * widened, axis=-1, keepdims=True) + epsilon)
    return widened * inverse * gain.astype(jnp.float32)


def rotate(vectors, angle_base):
    halfway = vectors.shape[-1] // 2
    spacing = jnp.arange(halfway, dtype=jnp.float32) / halfway
    freqs_all = jnp.exp(-jnp.log(10000.0) * spacing)
    angles = angle_base[:, None] * freqs_all[None, :]
    cosine = jnp.cos(angles)[:, None, :]
    sine_part = jnp.sin(angles)[:, None, :]
    leading = vectors[..., :halfway]
    trailing = vectors[..., halfway:]
    return jnp.concatenate(
        [leading * cosine - trailing * sine_part, trailing * cosine + leading * sine_part], axis=-1
    )


def doc_layout(seq_lengths, row_ids):
    ending = jnp.cumsum(seq_lengths, dtype=jnp.int32)
    passed = (ending[None, :] <= row_ids[:, None]).astype(jnp.int32)
    doc_ids = jnp.sum(passed, axis=1, dtype=jnp.int32)
    starting = jnp.sum(passed * seq_lengths[None, :], axis=1, dtype=jnp.int32)
    return (doc_ids, row_ids - starting)


def owner_table(placing):
    slot_range = jnp.arange(placing.shape[0], dtype=jnp.int32)
    return jnp.sum(
        jnp.where(placing[:, None] == slot_range[None, :], slot_range[:, None], 0),
        axis=0,
        dtype=jnp.int32,
    )


def attend_block(
    carried,
    queries,
    query_rows,
    query_docs,
    key_block,
    value_block,
    key_rows,
    seq_lengths,
    seen_row,
    block_rows,
):
    key_docs, _ = doc_layout(seq_lengths, key_rows)
    key_blocks = jnp.floor_divide(key_rows, block_rows)
    block_range = jnp.arange(seen_row.shape[0], dtype=jnp.int32)
    key_seen = (
        jnp.sum(
            jnp.where(key_blocks[:, None] == block_range[None, :], seen_row[None, :], 0),
            axis=1,
            dtype=jnp.int32,
        )
        > 0
    )
    allowed = (
        (query_docs[:, None] == key_docs[None, :])
        & (key_rows[None, :] <= query_rows[:, None])
        & key_seen[None, :]
    )
    score_scale = queries.shape[-1] ** (-0.5)

    def compute(state_in):
        largest, totals, summed = state_in
        scores = (
            jnp.einsum("qhd,khd->hqk", queries, key_block, preferred_element_type=jnp.float32)
            * score_scale
        )
        scores = jnp.where(allowed[None], scores, masked_score)
        new_largest = jnp.maximum(largest, jnp.max(scores, axis=2))
        weights = jnp.where(allowed[None], jnp.exp(scores - new_largest[:, :, None]), 0.0)
        totals = jnp.sum(weights, axis=2)
        summed = jnp.einsum(
            "hqk,khd->hqd",
            weights.astype(jnp.bfloat16),
            value_block,
            preferred_element_type=jnp.float32,
        )
        return (new_largest, totals, summed)

    def unchanged(state_in):
        return state_in

    return lax.cond(jnp.any(allowed), compute, unchanged, carried)


def shards(
    tokens,
    norm_gain,
    w_qkv,
    w_out,
    moe_gain,
    w_router,
    gate_up,
    w_down,
    lengths,
    blocks_seen,
    expert_ids,
    old_place,
    new_place,
):
    block_rows = tokens.shape[0]
    model_width = tokens.shape[1]
    exp_count = lax.axis_size("exp")
    block_index = lax.axis_index("seq")
    slot_index = lax.axis_index("exp")
    heads_here = w_qkv.shape[2] // HEAD_DIM
    query_rows = block_index * block_rows + jnp.arange(block_rows, dtype=jnp.int32)
    query_docs, query_places = doc_layout(lengths, query_rows)
    normed = rms_scale(tokens, norm_gain).astype(jnp.bfloat16)
    projected = jnp.dot(
        normed,
        w_qkv.reshape(model_width, 3 * heads_here * HEAD_DIM),
        preferred_element_type=jnp.float32,
    )
    projected = projected.reshape(block_rows, 3, heads_here, HEAD_DIM)
    angle_rows = query_places.astype(jnp.float32)
    queries = rotate(projected[:, 0], angle_rows).astype(jnp.bfloat16)
    key_block = rotate(projected[:, 1], angle_rows).astype(jnp.bfloat16)
    value_block = projected[:, 2].astype(jnp.bfloat16)
    seen_row = blocks_seen[0]
    initial = (
        jnp.full((heads_here, block_rows), masked_score, jnp.float32),
        jnp.zeros((heads_here, block_rows), jnp.float32),
        jnp.zeros((heads_here, block_rows, HEAD_DIM), jnp.float32),
    )
    pieces = (
        lax.all_gather(key_block, "seq", axis=0, tiled=True),
        lax.all_gather(value_block, "seq", axis=0, tiled=True),
    )
    key_rows = jnp.arange(pieces[0].shape[0], dtype=jnp.int32)
    largest, totals, summed = attend_block(
        initial,
        queries,
        query_rows,
        query_docs,
        pieces[0],
        pieces[1],
        key_rows,
        lengths,
        seen_row,
        block_rows,
    )
    attended = (summed / totals[:, :, None]).astype(jnp.bfloat16)
    attended = jnp.transpose(attended, (1, 0, 2)).reshape(block_rows, heads_here * HEAD_DIM)
    shard_rows = block_rows // exp_count
    rows_in = attended
    head_total = lax.psum_scatter(
        jnp.dot(rows_in, w_out, preferred_element_type=jnp.float32).astype(jnp.bfloat16),
        "exp",
        scatter_dimension=0,
        tiled=True,
    ).astype(jnp.float32)
    residual = lax.dynamic_slice_in_dim(tokens, slot_index * shard_rows, shard_rows, 0)
    hidden = (residual.astype(jnp.float32) + head_total).astype(jnp.bfloat16)
    moe_in = rms_scale(hidden, moe_gain).astype(jnp.bfloat16)
    logits = jnp.dot(moe_in, w_router, preferred_element_type=jnp.float32)
    expert_count = w_router.shape[1]
    expert_range = jnp.arange(expert_count, dtype=jnp.int32)
    chosen = jnp.sum(
        jnp.where(expert_ids[:, :, None] == expert_range[None, None, :], logits[:, None, :], 0.0),
        axis=2,
    )
    gate_first = 1.0 / (1.0 + jnp.exp(chosen[:, 1] - chosen[:, 0]))
    gate_second = 1.0 / (1.0 + jnp.exp(chosen[:, 0] - chosen[:, 1]))
    gating = jnp.stack([gate_first, gate_second], axis=1)
    slot_old = owner_table(old_place)
    source_slot = jnp.sum(
        jnp.where(new_place[:, None] == expert_range[None, :], slot_old[None, :], 0),
        axis=1,
        dtype=jnp.int32,
    )
    slice_width = gate_up.shape[3]
    piece_width = model_width // exp_count
    gate_split = gate_up.reshape(2, exp_count, piece_width, slice_width)
    down_split = w_down.reshape(slice_width, exp_count, piece_width)
    gate_held, down_held = (
        lax.all_to_all(gate_split, "exp", split_axis=1, concat_axis=1, tiled=True),
        lax.all_to_all(down_split, "exp", split_axis=1, concat_axis=1, tiled=True),
    )
    gate_sorted = jnp.take(gate_held, source_slot, axis=1)
    down_sorted = jnp.take(down_held, source_slot, axis=1)
    gate_moved, down_moved = (
        lax.all_to_all(gate_sorted, "exp", split_axis=1, concat_axis=1, tiled=True),
        lax.all_to_all(down_sorted, "exp", split_axis=1, concat_axis=1, tiled=True),
    )
    new_gate_up = gate_moved.reshape(1, 2, model_width, slice_width)
    new_down = down_moved.reshape(1, slice_width, model_width)
    owners = owner_table(new_place)
    column_gate = new_gate_up[0]
    column_down = new_down[0]
    capacity = min(shard_rows, 4 * shard_rows // exp_count)
    slot_total = exp_count * capacity
    pair_ids = expert_ids.reshape(-1)
    pair_marks = (pair_ids[:, None] == expert_range[None, :]).astype(jnp.int32)
    earlier = jnp.cumsum(pair_marks, axis=0, dtype=jnp.int32) - pair_marks
    rank_in = jnp.sum(earlier * pair_marks, axis=1, dtype=jnp.int32)
    owner_of = jnp.sum(pair_marks * owners[None, :], axis=1, dtype=jnp.int32)
    target = owner_of * capacity + rank_in
    selector = target[:, None] == jnp.arange(slot_total, dtype=jnp.int32)[None, :]
    repeated = jnp.repeat(moe_in, 2, axis=0)
    outgoing = jnp.einsum(
        "as,ad->sd", selector.astype(jnp.bfloat16), repeated, preferred_element_type=jnp.float32
    )
    outgoing = outgoing.astype(jnp.bfloat16).reshape(exp_count, capacity, model_width)
    arrived = lax.all_to_all(outgoing, "exp", split_axis=0, concat_axis=0, tiled=True)
    source_count = arrived.shape[0]
    item_count = arrived.shape[1]
    pieces = lax.all_gather(arrived, "seq", axis=0, tiled=True)
    flat_rows = pieces.reshape(-1, model_width)
    projected_pair = jnp.einsum(
        "rd,cdf->crf", flat_rows, column_gate, preferred_element_type=jnp.float32
    )
    activated = (jax.nn.silu(projected_pair[0]) * projected_pair[1]).astype(jnp.bfloat16)
    hidden_all = activated.reshape(pieces.shape[0], item_count, slice_width)
    rows_in = hidden_all
    flat_out = jnp.dot(
        rows_in.reshape(-1, slice_width), column_down, preferred_element_type=jnp.float32
    )
    column_sum = lax.psum_scatter(
        flat_out.reshape(source_count * lax.axis_size("seq"), item_count, model_width).astype(
            jnp.bfloat16
        ),
        "seq",
        scatter_dimension=0,
        tiled=True,
    )
    returned = lax.all_to_all(column_sum, "exp", split_axis=0, concat_axis=0, tiled=True)
    pair_gates = gating.reshape(-1)
    spread = jnp.sum(
        jnp.where(selector, pair_gates[:, None], 0.0).reshape(shard_rows, 2, slot_total), axis=1
    )
    moe_sum = jnp.dot(
        spread,
        returned.reshape(slot_total, model_width).astype(jnp.float32),
        precision=lax.Precision.HIGHEST,
    )
    layer_out = (hidden.astype(jnp.float32) + moe_sum).astype(jnp.bfloat16)
    return (layer_out, new_gate_up, new_down)


def solution(mesh):
    in_specs = (
        P("seq", None),
        P(),
        P(None, None, "exp"),
        P("exp", None),
        P(),
        P(),
        P("exp", None, None, "seq"),
        P("exp", "seq", None),
        P(),
        P("seq", None),
        P(("seq", "exp"), None),
        P(),
        P(),
    )
    out_specs = (P(("seq", "exp"), None), P("exp", None, None, "seq"), P("exp", "seq", None))
    return jax.shard_map(shards, mesh=mesh, in_specs=in_specs, out_specs=out_specs, check_vma=False)
```

profile of v0, /device:TPU:8, one launch (start us, length us, event | category | flops | bytes accessed | tf_op | source)
XLA Modules:
  0.0 512.6 jit_solution(13582045412710372037)
XLA Ops:
  7.3 1.3 fusion.20
  8.6 0.8 reduce-window.8
  9.4 0.7 fusion.39
  10.2 0.7 convert_element_type.85
  10.9 5.9 %copy.61 = bf16[2304,3,256]{0,2,1:T(8,128)(2,1)} copy(bf16[2304,3,256]{2,0,1:T(8,128)(2,1)} %param.17) | data formatting | bytes 7077888 | tf_op args[2]
  16.8 3.2 fusion.25
  20.0 0.1 multiply_cosine_fusion
  20.2 0.6 pad_maximum_fusion.1
  20.9 0.6 slice.79
  21.6 0.1 convert_reduce_fusion
  21.8 0.2 select_reduce_fusion
  21.9 1.6 fusion.41
  24.2 55.6 %all-gather.5.cloned.1.call-done = bf16[4096,4,64]{0,2,1:T(8,128)(2,1)} async-done(((bf16[128,4,64]{0,2,1:T(8,128)(2,1)}), bf16[4096,4,64]{0,2,1:T(8,128)(2,1)}) %all-gather.5.cloned.1.call-update) | async-done | bytes 2097168 | tf_op jit(solution)/shard_map/all_gather | solution.py:143
  79.8 56.4 %all-gather.9.cloned.1.call-done = bf16[4096,1,4,64]{0,3,2,1:T(8,128)(2,1)} async-done(((bf16[128,1,4,64]{0,3,2,1:T(8,128)(2,1)}), bf16[4096,1,4,64]{0,3,2,1:T(8,128)(2,1)}) %all-gather.9.cloned.1.call-update) | async-done | bytes 2097168 | tf_op jit(solution)/shard_map/all_gather | solution.py:144
  136.2 8.4 %conditional.1 = (f32[4,128]{1,0:T(4,128)S(1)}, f32[4,128,64]{1,2,0:T(8,128)S(1)}) conditional(s32[]{:T(128)} %convert_element_type.83, () %tuple.16, (pred[128,4096]{1,0:T(8,128)(4,1)S(1)}, bf16[128,4,64]{0,2,1:T(8,128)(2,1)S(1)}, bf16[4096,4,64]{0,2,1:T(8,128)(2,1)}, bf16[4096,4,64]{0,2,1:T(8,128)(2,1)}) %tuple.47), branch_computations={%region_7.8_spmd, %region_8.11_spmd} | conditional | flops 564133376 | bytes 39530540 | solution.py:99
  136.2 3.6 fusion
  139.8 2.3 fusion.3
  142.1 2.5 fusion.2
  144.7 1.2 convolution_convert_fusion
  146.0 0.1 copy.62
  146.1 0.1 eq.113
  146.3 0.1 select_reduce_fusion.6
  146.4 0.2 select_reduce_fusion.5
  146.6 0.2 select_reduce_fusion.3
  146.8 34.4 %reduce-scatter.5.cloned.1.call-done = bf16[16,2304]{1,0:T(8,128)(2,1)} async-done(((bf16[128,2304]{1,0:T(8,128)(2,1)}), bf16[16,2304]{1,0:T(8,128)(2,1)}) %reduce-scatter.5.cloned.1.call-update) | async-done | bytes 73744 | tf_op jit(solution)/shard_map/reduce_scatter | solution.py:163
  181.2 1.0 fusion.30
  182.2 0.1 fusion.32
  182.5 0.3 fusion.11
  182.8 12.7 %all_to_all.30 = bf16[8,8,2304]{2,1,0:T(8,128)(2,1)} all-to-all(bf16[8,8,2304]{2,1,0:T(8,128)(2,1)S(1)} %fusion.11), channel_id=1, replica_groups=mesh['seq'=32,'exp'=8] {'exp'}, dimensions={0} | all-to-all | bytes 589824 | tf_op jit(solution)/shard_map/all_to_all | solution.py:221
  195.5 1.7 reshape.231
  197.2 1.1 copy.68
  198.4 4.9 all-to-all-start.3
  203.3 5.4 %reshape.255 = bf16[2,8,288,180]{2,1,0,3:T(8,128)(2,1)S(1)} reshape(bf16[1,2,2304,180]{2,1,3,0:T(2,128)(2,1)} %param.21) | data formatting | bytes 3317760 | tf_op jit(solution)/shard_map/reshape | solution.py:190
  208.7 3.1 copy.65
  211.7 8.9 %all-to-all-done.3 = bf16[180,8,288]{2,0,1:T(8,128)(2,1)S(1)} async-done(((bf16[180,8,288]{2,0,1:T(8,128)(2,1)}), bf16[180,8,288]{2,0,1:T(8,128)(2,1)S(1)}, u32[]{:S(2)}, u32[]{:S(2)}) %all-to-all-start.3) | async-done | bytes 829472 | tf_op jit(solution)/shard_map/all_to_all | solution.py:194
  220.6 4.6 all-to-all-start
  225.3 1.7 gather_fusion.1
  227.0 2.4 select_bitcast_fusion
  229.5 52.2 %all-to-all-done = bf16[2,8,288,180]{2,0,3,1:T(2,128)(2,1)S(1)} async-done(((bf16[2,8,288,180]{2,0,3,1:T(2,128)(2,1)}), bf16[2,8,288,180]{2,0,3,1:T(2,128)(2,1)S(1)}, u32[]{:S(2)}, u32[]{:S(2)}) %all-to-all-start) | async-done | bytes 1658912 | tf_op jit(solution)/shard_map/all_to_all | solution.py:193
  281.7 6.3 %all-to-all-start.4 = ((bf16[180,8,288]{2,0,1:T(8,128)(2,1)}), bf16[180,8,288]{2,0,1:T(8,128)(2,1)S(1)}, u32[]{:S(2)}, u32[]{:S(2)}) async-start(bf16[180,8,288]{2,0,1:T(8,128)(2,1)} %select_bitcast_fusion), calls=%async_computation.5 | async-start | bytes 2260992 | tf_op jit(solution)/shard_map/all_to_all | solution.py:200
  288.0 6.3 %gather_fusion = bf16[8,2,288,180]{2,1,3,0:T(2,128)(2,1)} fusion(bf16[2,8,288,180]{2,0,3,1:T(2,128)(2,1)S(1)} %all-to-all-done, s32[1024]{0:T(1024)S(1)} %pad_clamp_fusion), kind=kCustom, calls=%fused_computation | custom fusion | bytes 3317792 | tf_op jit(solution)/shard_map/jit(_take)/gather | solution.py:196
  294.4 4.9 fusion.16
  299.3 6.4 %all-to-all-done.4 = bf16[180,8,288]{2,0,1:T(8,128)(2,1)S(1)} async-done(((bf16[180,8,288]{2,0,1:T(8,128)(2,1)}), bf16[180,8,288]{2,0,1:T(8,128)(2,1)S(1)}, u32[]{:S(2)}, u32[]{:S(2)}) %all-to-all-start.4) | async-done | bytes 829472 | tf_op jit(solution)/shard_map/all_to_all | solution.py:200
  305.7 1.0 copy-done.2
  306.7 6.2 %all-to-all-start.1 = ((bf16[2,8,288,180]{2,0,3,1:T(2,128)(2,1)}), bf16[2,8,288,180]{2,0,3,1:T(2,128)(2,1)S(1)}, u32[]{:S(2)}, u32[]{:S(2)}) async-start(bf16[2,8,288,180]{2,0,3,1:T(2,128)(2,1)} %fusion.16), calls=%async_computation.2 | async-start | bytes 4423680 | tf_op jit(solution)/shard_map/all_to_all | solution.py:199
  312.9 1.4 copy.69
  314.3 1.8 reshape.254
  316.1 12.4 %all-to-all-done.1 = bf16[2,8,288,180]{2,0,3,1:T(2,128)(2,1)S(1)} async-done(((bf16[2,8,288,180]{2,0,3,1:T(2,128)(2,1)}), bf16[2,8,288,180]{2,0,3,1:T(2,128)(2,1)S(1)}, u32[]{:S(2)}, u32[]{:S(2)}) %all-to-all-start.1) | async-done | bytes 1658912 | tf_op jit(solution)/shard_map/all_to_all | solution.py:199
  328.5 1.6 copy.66
  330.2 4.2 squeeze_reshape.6
  334.4 6.8 %fusion.13 = f32[2,2048,180]{1,2,0:T(8,128)S(1)} fusion(bf16[2,2304,180]{1,2,0:T(8,128)(2,1)} %squeeze_reshape.6, bf16[256,8,2304]{2,1,0:T(8,128)(2,1)} %all-gather.7.cloned.1.call-done), kind=kOutput, calls=%fused_computation.22 | convolution fusion | flops 3397386240 | bytes 14045184 | tf_op jit(solution)/shard_map/rd,cdf->crf/dot_general | solution.py:226
  341.2 1.3 fusion.19
  342.5 2.2 copy.67
  344.7 7.8 %convert_bitcast_fusion = bf16[8,32,8,2304]{3,2,1,0:T(8,128)(2,1)} fusion(bf16[180,2304,1]{1,0,2:T(8,128)(2,1)} %reshape.254, bf16[256,8,180]{2,1,0:T(8,128)(2,1)} %bitcast.73), kind=kOutput, calls=%fused_computation.15 | convolution fusion | flops 1703411712 | bytes 11003904 | tf_op jit(solution)/shard_map/dot_general | solution.py:232
  352.6 8.5 %copy.82 = bf16[8,32,8,2304]{3,2,0,1:T(8,128)(2,1)} copy(bf16[8,32,8,2304]{3,2,1,0:T(8,128)(2,1)} %convert_bitcast_fusion) | data formatting | bytes 18874368
  361.1 0.1 copy.63
  361.2 1.9 reshape.234
  363.1 0.1 fusion.43
  363.2 126.2 %reduce-scatter.7.cloned.1.call-done = bf16[8,18432]{1,0:T(8,128)(2,1)} async-done(((bf16[256,18432]{1,0:T(8,128)(2,1)}), bf16[8,18432]{1,0:T(8,128)(2,1)}) %reduce-scatter.7.cloned.1.call-update) | async-done | bytes 294928
  489.4 1.7 copy.71
  491.1 4.9 all-to-all-start.5
  496.1 1.8 copy.78
  498.0 6.3 %reshape.257 = bf16[1,2,2304,180]{2,1,3,0:T(2,128)(2,1)} reshape(bf16[2,8,288,180]{2,1,0,3:T(8,128)(2,1)} %copy.78) | data formatting | bytes 3317760
  504.2 1.8 fusion.12
  (61 shorter events, 1.0 us)
Async XLA Ops:
  7.2 137.5 %copy-start = (bf16[256,2304]{1,0:T(8,128)(2,1)S(1)}, bf16[256,2304]{1,0:T(8,128)(2,1)}, u32[]{:S(2)}) copy-start(bf16[256,2304]{1,0:T(8,128)(2,1)} %param.18) | copy-start | bytes 3538948
  7.2 72.6 %all-gather.5.cloned.1.call-start = ((), (), s32[]{:S(2)}) async-start(), calls=%async_computation.8 | async-start | bytes 2162688 | tf_op jit(solution)/shard_map/all_gather | solution.py:143
  10.9 5.9 %copy-start.3 = (bf16[128,2304]{1,0:T(8,128)(2,1)S(1)}, bf16[128,2304]{1,0:T(8,128)(2,1)}, u32[]{:S(2)}) copy-start(bf16[128,2304]{1,0:T(8,128)(2,1)} %param.15) | copy-start | bytes 1769476
  16.8 5.0 copy-start.8
  20.8 115.4 %all-gather.9.cloned.1.call-start = ((), (), s32[]{:S(2)}) async-start(), calls=%async_computation.11 | async-start | bytes 2162688 | tf_op jit(solution)/shard_map/all_gather | solution.py:144
  21.6 159.6 %reduce-scatter.5.cloned.1.call-start = ((), (), s32[]{:S(2)}) async-start(), calls=%async_computation.9 | async-start | bytes 663552 | tf_op jit(solution)/shard_map/reduce_scatter | solution.py:163
  136.2 3.6 copy-start.10
  144.6 1.3 copy-start.7
  144.6 1.5 copy-start.6
  144.6 1.7 copy-start.11
  144.7 1.7 copy-start.9
  144.7 50.8 %copy-start.4 = (bf16[1,180,2304]{2,1,0:T(8,128)(2,1)S(1)}, bf16[1,180,2304]{2,1,0:T(8,128)(2,1)}, u32[]{:S(2)}) copy-start(bf16[1,180,2304]{2,1,0:T(8,128)(2,1)} %param.22) | copy-start | bytes 2488324
  145.9 188.5 %all-gather.7.cloned.1.call-start = ((), (), s32[]{:S(2)}) async-start(), calls=%async_computation.10 | async-start | bytes 9732096 | tf_op jit(solution)/shard_map/all_gather | solution.py:224
  198.4 22.3 %all-to-all-start.3 = ((bf16[180,8,288]{2,0,1:T(8,128)(2,1)}), bf16[180,8,288]{2,0,1:T(8,128)(2,1)S(1)}, u32[]{:S(2)}, u32[]{:S(2)}) async-start(bf16[180,8,288]{2,0,1:T(8,128)(2,1)} %copy.68), calls=%async_computation.4 | async-start | bytes 2260992 | tf_op jit(solution)/shard_map/all_to_all | solution.py:194
  220.6 61.0 %all-to-all-start = ((bf16[2,8,288,180]{2,0,3,1:T(2,128)(2,1)}), bf16[2,8,288,180]{2,0,3,1:T(2,128)(2,1)S(1)}, u32[]{:S(2)}, u32[]{:S(2)}) async-start(bf16[2,8,288,180]{2,0,3,1:T(2,128)(2,1)} %copy.65), calls=%async_computation.1 | async-start | bytes 4423680 | tf_op jit(solution)/shard_map/all_to_all | solution.py:193
  281.7 24.0 %all-to-all-start.4 = ((bf16[180,8,288]{2,0,1:T(8,128)(2,1)}), bf16[180,8,288]{2,0,1:T(8,128)(2,1)S(1)}, u32[]{:S(2)}, u32[]{:S(2)}) async-start(bf16[180,8,288]{2,0,1:T(8,128)(2,1)} %select_bitcast_fusion), calls=%async_computation.5 | async-start | bytes 2260992 | tf_op jit(solution)/shard_map/all_to_all | solution.py:200
  305.7 1.0 copy-start.2
  306.7 21.8 %all-to-all-start.1 = ((bf16[2,8,288,180]{2,0,3,1:T(2,128)(2,1)}), bf16[2,8,288,180]{2,0,3,1:T(2,128)(2,1)S(1)}, u32[]{:S(2)}, u32[]{:S(2)}) async-start(bf16[2,8,288,180]{2,0,3,1:T(2,128)(2,1)} %fusion.16), calls=%async_computation.2 | async-start | bytes 4423680 | tf_op jit(solution)/shard_map/all_to_all | solution.py:199
  312.9 176.6 %reduce-scatter.7.cloned.1.call-start = ((), (), s32[]{:S(2)}) async-start(), calls=%async_computation.12 | async-start | bytes 9732096
  361.0 2.0 copy-start.5
  491.1 13.1 %all-to-all-start.5 = ((bf16[8,8,2304]{2,1,0:T(8,128)(2,1)}), bf16[8,8,2304]{2,1,0:T(8,128)(2,1)}, u32[]{:S(2)}, u32[]{:S(2)}) async-start(bf16[8,8,2304]{2,1,0:T(8,128)(2,1)} %copy.71), calls=%async_computation.6 | async-start | bytes 589824 | tf_op jit(solution)/shard_map/all_to_all | solution.py:243
  496.1 10.0 %copy-start.1 = (bf16[256,2304]{1,0:T(8,128)(2,1)S(1)}, bf16[256,2304]{1,0:T(8,128)(2,1)}, u32[]{:S(2)}) copy-start(bf16[256,2304]{1,0:T(8,128)(2,1)} %param.18) | copy-start | bytes 3538948
Sparse Core Ops, SparseCore 0:
  20.9 58.7 all-gather.4
  82.8 53.3 all-gather.8
  146.0 35.1 reduce-scatter.4
  195.6 97.8 all-gather.6
  361.2 128.2 reduce-scatter.6
where the time goes:
time: 514 us; the launch traced here: 513 us
  waiting for transfers between devices  353 us (69%)
  local copies, waits for them, and re-layouts  58.8 us (11%)
  matrix products  27.2 us (5%)
  starting transfers between devices  27.1 us (5%)
  other arithmetic  19.4 us (4%)
  between operations  14.7 us (3%)
  blocking collectives  12.7 us (2%)
    unnamed x6, waiting for transfers between devices  126 us
    all_gather x1, waiting for transfers between devices, shards(): lax.all_gather(value_block, 'seq', axis=0, tiled=True)  56.4 us
    all_gather x1, waiting for transfers between devices, shards(): lax.all_gather(key_block, 'seq', axis=0, tiled=True)  55.6 us
    all_to_all x1, waiting for transfers between devices, shards(): lax.all_to_all(gate_split, 'exp', split_axis=1, concat_axis=1, tiled=True)  52.2 us
    reduce_scatter x1, waiting for transfers between devices, shards(): lax.psum_scatter(jnp.dot(rows_in, w_out, preferred_element_type=jnp.float...  34.4 us
    unnamed x27, local copies, waits for them, and re-layouts  23.6 us
    all_to_all x1, blocking collectives, shards(): lax.all_to_all(outgoing, 'exp', split_axis=0, concat_axis=0, tiled=True)  12.7 us
    all_to_all x1, waiting for transfers between devices, shards(): lax.all_to_all(gate_sorted, 'exp', split_axis=1, concat_axis=1, tiled=True)  12.4 us
  transfers between devices with their start and end apart: 10, of which 8 were waited for; matrix products, arithmetic and copies ran while one was open for 10% of the time, Pallas kernels for 0%

commit v1 on v0

--- a/solution.py
+++ b/solution.py
@@ -6,6 +6,11 @@
 HEAD_DIM = 64
 epsilon = 1e-05
 masked_score = -1e30
+
+
+def swapped_in(shard, axis, dim):
+    outgoing = jnp.stack([shard] * lax.axis_size(axis))
+    return jnp.concatenate(lax.all_to_all(outgoing, axis, 0, 0), axis=dim)
 
 
 def rms_scale(values_in, gain):
@@ -140,7 +145,7 @@
         jnp.zeros((heads_here, block_rows, HEAD_DIM), jnp.float32),
     )
     pieces = (
-        lax.all_gather(key_block, "seq", axis=0, tiled=True),
+        swapped_in(key_block, "seq", 0),
         lax.all_gather(value_block, "seq", axis=0, tiled=True),
     )
     key_rows = jnp.arange(pieces[0].shape[0], dtype=jnp.int32)

time: 514 us -> 475 us (0.924)
  waiting for transfers between devices: 353 us -> 299 us
  starting transfers between devices: 27.1 us -> 42.8 us
    all_gather x1 -> x0, waiting for transfers between devices: 55.6 us -> none  [shards(): lax.all_gather(key_block, 'seq', axis=0, tiled=True)]
    all_to_all x0 -> x1, starting transfers between devices: none -> 11.4 us  [swapped_in(): return jnp.concatenate(lax.all_to_all(outgoing, axis, 0, 0), axis=dim)]
    unnamed x6 -> x5, waiting for transfers between devices: 126 us -> 127 us
    unnamed x27 -> x29, local copies, waits for them, and re-layouts: 23.6 us -> 23.6 us
  transfers between devices with their start and end apart: 10 -> 10, of which waited for: 8 -> 7; matrix products, arithmetic and copies ran while one was open for 10% -> 11% of each run, Pallas kernels for 0% -> 0%
where the time goes in v1:
time: 475 us; the launch traced here: 474 us
  waiting for transfers between devices  299 us (63%)
  local copies, waits for them, and re-layouts  60.7 us (13%)
  starting transfers between devices  42.8 us (9%)
  matrix products  26.5 us (6%)
  other arithmetic  18 us (4%)
  between operations  14.7 us (3%)
  blocking collectives  12.5 us (3%)
    unnamed x5, waiting for transfers between devices  127 us
    all_gather x1, waiting for transfers between devices, shards(): lax.all_gather(value_block, 'seq', axis=0, tiled=True)  60.1 us
    all_to_all x1, waiting for transfers between devices, shards(): lax.all_to_all(gate_split, 'exp', split_axis=1, concat_axis=1, tiled=True)  52.1 us
    reduce_scatter x1, waiting for transfers between devices, shards(): lax.psum_scatter(jnp.dot(rows_in, w_out, preferred_element_type=jnp.float...  37 us
    unnamed x29, local copies, waits for them, and re-layouts  23.6 us
    all_to_all x1, blocking collectives, shards(): lax.all_to_all(outgoing, 'exp', split_axis=0, concat_axis=0, tiled=True)  12.5 us
    all_to_all x1, waiting for transfers between devices, shards(): lax.all_to_all(gate_sorted, 'exp', split_axis=1, concat_axis=1, tiled=True)  12.4 us
    all_to_all x1, starting transfers between devices, swapped_in(): return jnp.concatenate(lax.all_to_all(outgoing, axis, 0, 0), axis=dim)  11.4 us
  transfers between devices with their start and end apart: 10, of which 7 were waited for; matrix products, arithmetic and copies ran while one was open for 11% of the time, Pallas kernels for 0%

profile of v1, /device:TPU:8, one launch (start us, length us, event | category | flops | bytes accessed | tf_op | source)
XLA Modules:
  0.0 474.3 jit_solution(297042093473740062)
XLA Ops:
  7.2 1.4 fusion.23
  8.6 0.7 convert_element_type.87
  9.3 5.9 %copy.62 = bf16[2304,3,256]{0,2,1:T(8,128)(2,1)} copy(bf16[2304,3,256]{2,0,1:T(8,128)(2,1)} %param.17) | data formatting | bytes 7077888 | tf_op args[2]
  15.2 3.2 fusion.28
  18.3 0.6 slice.79
  19.1 0.2 reduce-window.8
  19.3 0.1 fusion.42
  19.4 0.1 multiply_cosine_fusion
  19.6 1.8 stack.4
  21.4 11.4 %all-to-all-start = ((bf16[32,128,4,64]{1,3,2,0:T(8,128)(2,1)}), bf16[32,128,4,64]{1,3,2,0:T(8,128)(2,1)S(1)}, u32[]{:S(2)}, u32[]{:S(2)}) async-start(bf16[32,128,4,64]{1,3,2,0:T(8,128)(2,1)} %stack.4), calls=%async_computation | async-start | bytes 4194304 | tf_op jit(solution)/shard_map/all_to_all | solution.py:13
  32.9 0.1 convert_reduce_fusion
  33.0 0.2 select_reduce_fusion
  33.2 2.0 fusion.44
  35.9 60.1 %all-gather.6.cloned.1.call-done = bf16[4096,1,4,64]{0,3,2,1:T(8,128)(2,1)} async-done(((bf16[128,1,4,64]{0,3,2,1:T(8,128)(2,1)}), bf16[4096,1,4,64]{0,3,2,1:T(8,128)(2,1)}) %all-gather.6.cloned.1.call-update) | async-done | bytes 2097168 | tf_op jit(solution)/shard_map/all_gather | solution.py:149
  96.0 7.7 %conditional.1 = (f32[4,128]{1,0:T(4,128)S(1)}, f32[4,128,64]{1,2,0:T(8,128)S(1)}) conditional(s32[]{:T(128)} %convert_element_type.85, () %tuple.16, (pred[128,4096]{1,0:T(8,128)(4,1)}, bf16[32,128,4,64]{1,3,2,0:T(8,128)(2,1)S(1)}, bf16[128,4,64]{0,2,1:T(8,128)(2,1)S(1)}, bf16[4096,4,64]{0,2,1:T(8,128)(2,1)}) %tuple.47), branch_computations={%region_7.8_spmd, %region_8.11_spmd} | conditional | flops 564133376 | bytes 41627720 | solution.py:104
  96.1 2.9 fusion
  98.9 2.3 fusion.3
  101.3 2.5 fusion.2
  103.9 1.2 convolution_convert_fusion
  105.1 0.1 copy.64
  105.2 0.1 eq.113
  105.5 0.1 select_reduce_fusion.6
  105.5 0.2 select_reduce_fusion.5
  105.7 0.2 select_reduce_fusion.3
  105.9 37.0 %reduce-scatter.5.cloned.1.call-done = bf16[16,2304]{1,0:T(8,128)(2,1)} async-done(((bf16[128,2304]{1,0:T(8,128)(2,1)}), bf16[16,2304]{1,0:T(8,128)(2,1)}) %reduce-scatter.5.cloned.1.call-update) | async-done | bytes 73744 | tf_op jit(solution)/shard_map/reduce_scatter | solution.py:168
  142.9 1.1 fusion.33
  144.0 0.1 fusion.35
  144.3 0.3 fusion.14
  144.6 12.5 %all_to_all.35 = bf16[8,8,2304]{2,1,0:T(8,128)(2,1)} all-to-all(bf16[8,8,2304]{2,1,0:T(8,128)(2,1)S(1)} %fusion.14), channel_id=1, replica_groups=mesh['seq'=32,'exp'=8] {'exp'}, dimensions={0} | all-to-all | bytes 589824 | tf_op jit(solution)/shard_map/all_to_all | solution.py:226
  157.2 1.7 reshape.242
  158.9 1.1 copy.70
  160.0 4.9 %all-to-all-start.4 = ((bf16[180,8,288]{2,0,1:T(8,128)(2,1)}), bf16[180,8,288]{2,0,1:T(8,128)(2,1)S(1)}, u32[]{:S(2)}, u32[]{:S(2)}) async-start(bf16[180,8,288]{2,0,1:T(8,128)(2,1)} %copy.70), calls=%async_computation.5 | async-start | bytes 2260992 | tf_op jit(solution)/shard_map/all_to_all | solution.py:199
  164.9 5.4 %reshape.266 = bf16[2,8,288,180]{2,1,0,3:T(8,128)(2,1)S(1)} reshape(bf16[1,2,2304,180]{2,1,3,0:T(2,128)(2,1)} %param.21) | data formatting | bytes 3317760 | tf_op jit(solution)/shard_map/reshape | solution.py:195
  170.3 3.1 copy.67
  173.4 8.9 %all-to-all-done.4 = bf16[180,8,288]{2,0,1:T(8,128)(2,1)S(1)} async-done(((bf16[180,8,288]{2,0,1:T(8,128)(2,1)}), bf16[180,8,288]{2,0,1:T(8,128)(2,1)S(1)}, u32[]{:S(2)}, u32[]{:S(2)}) %all-to-all-start.4) | async-done | bytes 829472 | tf_op jit(solution)/shard_map/all_to_all | solution.py:199
  182.3 4.6 all-to-all-start.1
  186.9 1.7 gather_fusion.1
  188.6 2.4 select_bitcast_fusion
  191.1 52.1 %all-to-all-done.1 = bf16[2,8,288,180]{2,0,3,1:T(2,128)(2,1)S(1)} async-done(((bf16[2,8,288,180]{2,0,3,1:T(2,128)(2,1)}), bf16[2,8,288,180]{2,0,3,1:T(2,128)(2,1)S(1)}, u32[]{:S(2)}, u32[]{:S(2)}) %all-to-all-start.1) | async-done | bytes 1658912 | tf_op jit(solution)/shard_map/all_to_all | solution.py:198
  243.1 6.3 %all-to-all-start.5 = ((bf16[180,8,288]{2,0,1:T(8,128)(2,1)}), bf16[180,8,288]{2,0,1:T(8,128)(2,1)S(1)}, u32[]{:S(2)}, u32[]{:S(2)}) async-start(bf16[180,8,288]{2,0,1:T(8,128)(2,1)} %select_bitcast_fusion), calls=%async_computation.6 | async-start | bytes 2260992 | tf_op jit(solution)/shard_map/all_to_all | solution.py:205
  249.5 6.3 %gather_fusion = bf16[8,2,288,180]{2,1,3,0:T(2,128)(2,1)} fusion(bf16[2,8,288,180]{2,0,3,1:T(2,128)(2,1)S(1)} %all-to-all-done.1, s32[1024]{0:T(1024)S(1)} %pad_clamp_fusion), kind=kCustom, calls=%fused_computation | custom fusion | bytes 3317792 | tf_op jit(solution)/shard_map/jit(_take)/gather | solution.py:201
  255.8 4.9 %fusion.19 = bf16[2,8,288,180]{2,0,3,1:T(2,128)(2,1)} fusion(bf16[8,2,288,180]{2,1,3,0:T(2,128)(2,1)} %gather_fusion, pred[8]{0:T(512)(128)(4,1)S(1)} %compare_and_fusion), kind=kLoop, calls=%fused_computation.26 | loop fusion | flops 829440 | bytes 3317768 | tf_op jit(solution)/shard_map/jit(_take)/select_n | solution.py:201
  260.8 2.1 all-to-all-done.5
  262.8 1.0 copy-done.3
  263.8 10.5 %all-to-all-start.2 = ((bf16[2,8,288,180]{2,0,3,1:T(2,128)(2,1)}), bf16[2,8,288,180]{2,0,3,1:T(2,128)(2,1)S(1)}, u32[]{:S(2)}, u32[]{:S(2)}) async-start(bf16[2,8,288,180]{2,0,3,1:T(2,128)(2,1)} %fusion.19), calls=%async_computation.3 | async-start | bytes 4423680 | tf_op jit(solution)/shard_map/all_to_all | solution.py:204
  274.3 1.4 copy.71
  275.7 1.8 reshape.265
  277.6 12.4 %all-to-all-done.2 = bf16[2,8,288,180]{2,0,3,1:T(2,128)(2,1)S(1)} async-done(((bf16[2,8,288,180]{2,0,3,1:T(2,128)(2,1)}), bf16[2,8,288,180]{2,0,3,1:T(2,128)(2,1)S(1)}, u32[]{:S(2)}, u32[]{:S(2)}) %all-to-all-start.2) | async-done | bytes 1658912 | tf_op jit(solution)/shard_map/all_to_all | solution.py:204
  290.0 1.6 copy.68
  291.6 4.2 squeeze_reshape.6
  295.8 6.8 %fusion.16 = f32[2,2048,180]{1,2,0:T(8,128)S(1)} fusion(bf16[2,2304,180]{1,2,0:T(8,128)(2,1)} %squeeze_reshape.6, bf16[256,8,2304]{2,1,0:T(8,128)(2,1)} %all-gather.4.cloned.1.call-done), kind=kOutput, calls=%fused_computation.25 | convolution fusion | flops 3397386240 | bytes 14045184 | tf_op jit(solution)/shard_map/rd,cdf->crf/dot_general | solution.py:231
  302.7 1.3 fusion.22
  304.0 2.2 copy.69
  306.2 7.8 %convert_bitcast_fusion = bf16[8,32,8,2304]{3,2,1,0:T(8,128)(2,1)} fusion(bf16[180,2304,1]{1,0,2:T(8,128)(2,1)} %reshape.265, bf16[256,8,180]{2,1,0:T(8,128)(2,1)} %bitcast.81), kind=kOutput, calls=%fused_computation.18 | convolution fusion | flops 1703411712 | bytes 11003904 | tf_op jit(solution)/shard_map/dot_general | solution.py:237
  314.0 8.5 %copy.85 = bf16[8,32,8,2304]{3,2,0,1:T(8,128)(2,1)} copy(bf16[8,32,8,2304]{3,2,1,0:T(8,128)(2,1)} %convert_bitcast_fusion) | data formatting | bytes 18874368
  322.6 0.1 copy.65
  322.7 1.9 reshape.245
  324.5 0.1 fusion.46
  324.7 126.5 %reduce-scatter.7.cloned.1.call-done = bf16[8,18432]{1,0:T(8,128)(2,1)} async-done(((bf16[256,18432]{1,0:T(8,128)(2,1)}), bf16[8,18432]{1,0:T(8,128)(2,1)}) %reduce-scatter.7.cloned.1.call-update) | async-done | bytes 294928
  451.1 1.7 copy.73
  452.8 4.8 %all-to-all-start.6 = ((bf16[8,8,2304]{2,1,0:T(8,128)(2,1)}), bf16[8,8,2304]{2,1,0:T(8,128)(2,1)}, u32[]{:S(2)}, u32[]{:S(2)}) async-start(bf16[8,8,2304]{2,1,0:T(8,128)(2,1)} %copy.73), calls=%async_computation.7 | async-start | bytes 589824 | tf_op jit(solution)/shard_map/all_to_all | solution.py:248
  457.8 1.8 copy.80
  459.6 6.3 %reshape.268 = bf16[1,2,2304,180]{2,1,3,0:T(2,128)(2,1)} reshape(bf16[2,8,288,180]{2,1,0,3:T(8,128)(2,1)} %copy.80) | data formatting | bytes 3317760
  465.9 1.8 fusion.15
  (65 shorter events, 0.9 us)
Async XLA Ops:
  7.2 96.7 %copy-start = (bf16[256,2304]{1,0:T(8,128)(2,1)S(1)}, bf16[256,2304]{1,0:T(8,128)(2,1)}, u32[]{:S(2)}) copy-start(bf16[256,2304]{1,0:T(8,128)(2,1)} %param.18) | copy-start | bytes 3538948
  7.2 88.9 %all-gather.6.cloned.1.call-start = ((), (), s32[]{:S(2)}) async-start(), calls=%async_computation.11 | async-start | bytes 2162688 | tf_op jit(solution)/shard_map/all_gather | solution.py:149
  9.3 5.9 %copy-start.4 = (bf16[128,2304]{1,0:T(8,128)(2,1)S(1)}, bf16[128,2304]{1,0:T(8,128)(2,1)}, u32[]{:S(2)}) copy-start(bf16[128,2304]{1,0:T(8,128)(2,1)} %param.15) | copy-start | bytes 1769476
  15.2 3.9 copy-start.10
  21.4 11.6 %copy-start.9 = (s32[1,32]{1,0:T(1,128)S(1)}, s32[1,32]{1,0:T(1,128)}, u32[]{:S(2)}) copy-start(s32[1,32]{1,0:T(1,128)} %param.24) | copy-start | bytes 388
  21.4 74.7 %all-to-all-start = ((bf16[32,128,4,64]{1,3,2,0:T(8,128)(2,1)}), bf16[32,128,4,64]{1,3,2,0:T(8,128)(2,1)S(1)}, u32[]{:S(2)}, u32[]{:S(2)}) async-start(bf16[32,128,4,64]{1,3,2,0:T(8,128)(2,1)} %stack.4), calls=%async_computation | async-start | bytes 4194304 | tf_op jit(solution)/shard_map/all_to_all | solution.py:13
  32.8 110.1 %reduce-scatter.5.cloned.1.call-start = ((), (), s32[]{:S(2)}) async-start(), calls=%async_computation.9 | async-start | bytes 663552 | tf_op jit(solution)/shard_map/reduce_scatter | solution.py:168
  96.0 2.9 copy-start.2
  96.1 2.9 copy-start.12
  103.8 1.3 copy-start.8
  103.8 1.5 copy-start.7
  103.8 1.7 copy-start.13
  103.8 1.7 copy-start.11
  103.9 53.3 %copy-start.5 = (bf16[1,180,2304]{2,1,0:T(8,128)(2,1)S(1)}, bf16[1,180,2304]{2,1,0:T(8,128)(2,1)}, u32[]{:S(2)}) copy-start(bf16[1,180,2304]{2,1,0:T(8,128)(2,1)} %param.22) | copy-start | bytes 2488324
  105.1 190.8 %all-gather.4.cloned.1.call-start = ((), (), s32[]{:S(2)}) async-start(), calls=%async_computation.10 | async-start | bytes 9732096 | tf_op jit(solution)/shard_map/all_gather | solution.py:229
  160.0 22.3 %all-to-all-start.4 = ((bf16[180,8,288]{2,0,1:T(8,128)(2,1)}), bf16[180,8,288]{2,0,1:T(8,128)(2,1)S(1)}, u32[]{:S(2)}, u32[]{:S(2)}) async-start(bf16[180,8,288]{2,0,1:T(8,128)(2,1)} %copy.70), calls=%async_computation.5 | async-start | bytes 2260992 | tf_op jit(solution)/shard_map/all_to_all | solution.py:199
  182.3 60.9 %all-to-all-start.1 = ((bf16[2,8,288,180]{2,0,3,1:T(2,128)(2,1)}), bf16[2,8,288,180]{2,0,3,1:T(2,128)(2,1)S(1)}, u32[]{:S(2)}, u32[]{:S(2)}) async-start(bf16[2,8,288,180]{2,0,3,1:T(2,128)(2,1)} %copy.67), calls=%async_computation.2 | async-start | bytes 4423680 | tf_op jit(solution)/shard_map/all_to_all | solution.py:198
  243.1 19.7 %all-to-all-start.5 = ((bf16[180,8,288]{2,0,1:T(8,128)(2,1)}), bf16[180,8,288]{2,0,1:T(8,128)(2,1)S(1)}, u32[]{:S(2)}, u32[]{:S(2)}) async-start(bf16[180,8,288]{2,0,1:T(8,128)(2,1)} %select_bitcast_fusion), calls=%async_computation.6 | async-start | bytes 2260992 | tf_op jit(solution)/shard_map/all_to_all | solution.py:205
  262.8 1.0 copy-start.3
  263.8 26.2 %all-to-all-start.2 = ((bf16[2,8,288,180]{2,0,3,1:T(2,128)(2,1)}), bf16[2,8,288,180]{2,0,3,1:T(2,128)(2,1)S(1)}, u32[]{:S(2)}, u32[]{:S(2)}) async-start(bf16[2,8,288,180]{2,0,3,1:T(2,128)(2,1)} %fusion.19), calls=%async_computation.3 | async-start | bytes 4423680 | tf_op jit(solution)/shard_map/all_to_all | solution.py:204
  274.3 176.8 %reduce-scatter.7.cloned.1.call-start = ((), (), s32[]{:S(2)}) async-start(), calls=%async_computation.12 | async-start | bytes 9732096
  322.5 2.0 copy-start.6
  452.8 13.1 %all-to-all-start.6 = ((bf16[8,8,2304]{2,1,0:T(8,128)(2,1)}), bf16[8,8,2304]{2,1,0:T(8,128)(2,1)}, u32[]{:S(2)}, u32[]{:S(2)}) async-start(bf16[8,8,2304]{2,1,0:T(8,128)(2,1)} %copy.73), calls=%async_computation.7 | async-start | bytes 589824 | tf_op jit(solution)/shard_map/all_to_all | solution.py:248
  457.8 10.0 %copy-start.1 = (bf16[256,2304]{1,0:T(8,128)(2,1)S(1)}, bf16[256,2304]{1,0:T(8,128)(2,1)}, u32[]{:S(2)}) copy-start(bf16[256,2304]{1,0:T(8,128)(2,1)} %param.18) | copy-start | bytes 3538948
Sparse Core Ops, SparseCore 0:
  19.1 76.8 all-gather.5
  105.2 37.7 reduce-scatter.4
  157.3 97.7 all-gather.3
  322.6 128.4 reduce-scatter.6
